TPU v7x, 32 devices: a whole 2x2x4 slice. The times are simulated.
32 devices in a mesh: dp: 8 (over y, x, core), space: 4 (over z).
Axes of the slice: x: 2, y: 2, z: 4, core: 2. Of those that a mesh axis runs over, the one named last changes fastest.
Arguments:
- inputs: bfloat16 [64, 32, 32, 1024], P('dp', None, 'space'), may hold values from 0 to 2
- conv_in: bfloat16 [64, 864], replicated, may hold values from -0.21875 to 0.21875
- norm_gain: float32 [64], replicated, may hold values from 0.5 to 1.5
- norm_shift: float32 [64], replicated, may hold values from -3 to 3
- conv_out: bfloat16 [128, 1728], replicated, may hold values from -0.15625 to 0.15625
- dense_in: bfloat16 [65536, 128], replicated, may hold values from -0.0234375 to 0.0234375
- dense_out: bfloat16 [128, 4], replicated, may hold values from -0.5 to 0.5
- targets: float32 [64, 4], P(('dp', 'space')), may hold values from -6 to 6
Outputs:
- grad_conv_in: float32 [64, 864], replicated
- grad_norm: float32 [2, 64], replicated
- grad_conv_out: float32 [128, 1728], replicated
- grad_dense_in: float32 [65536, 128], P(('dp', 'space'))
- grad_dense_out: float32 [128, 4], replicated
- predictions: float32 [64, 4], P(('dp', 'space'))
All inputs are finite; a program needn't handle non-finite values.
Results may differ from a plain program's by a relative error of at most 0.015.
Values may be sent and summed in bfloat16 or wider, within the bound.
No kernel may reach another device: no remote copies, remote signals or barrier semaphores. Data moves between devices by JAX's collectives and lax.ppermute only.
A program may use at most 256 MiB of HBM per device.

v0:
```python
import jax
import jax.numpy as jnp
from jax import lax
from jax.sharding import PartitionSpec as P

C_OUT = 128
GRID = 32
norm_epsilon = 1e-05


def extended_2(cells, sides, width):
    for axis, dim in sides:
        count = lax.axis_size(axis)
        ends = count - 1
        head = lax.slice_in_dim(cells, 0, width, axis=dim)
        tail = lax.slice_in_dim(cells, cells.shape[dim] - width, cells.shape[dim], axis=dim)
        cells = jnp.concatenate(
            [
                lax.ppermute(tail, axis, [(i, (i + 1) % count) for i in range(ends)]),
                cells,
                lax.ppermute(head, axis, [((i + 1) % count, i) for i in range(ends)]),
            ],
            axis=dim,
        )
    return cells


def leaky_relu(values):
    return 0.65 * values + 0.35 * values * jnp.tanh(values)


def slope_of(values):
    bent = jnp.tanh(values)
    return 0.65 + 0.35 * (bent + values * (1.0 - bent * bent))


def plane_shift(volume, step_y, step_z, extent):
    plane_len = extent * extent
    offset = step_y * extent + step_z
    margin = extent + 1
    pad_widths = [(0, 0)] * (volume.ndim - 1) + [(margin, margin)]
    padded = jnp.pad(volume, pad_widths)
    shifted = lax.slice_in_dim(
        padded, margin + offset, margin + offset + plane_len, axis=volume.ndim - 1
    )
    column = lax.broadcasted_iota(jnp.int32, (plane_len,), 0) % extent
    inside = ((column + step_z >= 0) & (column + step_z < extent)).astype(volume.dtype)
    return shifted * inside


def columns(slab_ext, planes, extent):
    pieces = []
    for step_x in (-1, 0, 1):
        plane_set = lax.slice_in_dim(slab_ext, 1 + step_x, 1 + step_x + planes, axis=1)
        for step_y in (-1, 0, 1):
            for step_z in (-1, 0, 1):
                pieces.append(plane_shift(plane_set, step_y, step_z, extent))
    stacked = jnp.stack(pieces, 0)
    return stacked.reshape(len(pieces) * slab_ext.shape[0], planes * extent * extent)


def pad_planes(volume, extent):
    shaped = volume.reshape(volume.shape[0], extent, extent * extent)
    return jnp.pad(shaped, ((0, 0), (1, 1), (0, 0)))


def pool_slab(active, planes, extent):
    samples, channels = (active.shape[0], active.shape[1])
    blocks = active.reshape(samples, channels, planes // 2, 2, extent // 2, 2, extent // 2, 2)
    return (blocks.sum(axis=(3, 5, 7)) * 0.125).reshape(samples, channels, -1)


def unpool_slab(gradient, planes, extent):
    samples, channels = (gradient.shape[0], gradient.shape[1])
    blocks = gradient.reshape(samples, channels, planes // 2, 1, extent // 2, 1, extent // 2, 1)
    wide = jnp.broadcast_to(
        blocks, (samples, channels, planes // 2, 2, extent // 2, 2, extent // 2, 2)
    )
    return wide.reshape(samples, channels, planes * extent * extent) * 0.125


def shards(inputs, conv_in, norm_gain, norm_shift, conv_out, dense_in, dense_out, targets):
    half_grid = GRID // 2
    quarter = GRID // 4
    cell_count = inputs.shape[0] * GRID**3
    extended = extended_2(inputs, (("space", 2),), 1)
    planes = extended.shape[2] - 2

    def first_conv(slab_ext):
        return jnp.dot(conv_in, columns(slab_ext, planes, GRID), preferred_element_type=jnp.float32)

    first_out = lax.map(first_conv, extended)
    local_sum = jnp.sum(first_out, axis=(0, 2))
    average = lax.psum(local_sum, "space") / cell_count
    centred = first_out - average[None, :, None]
    variance = lax.psum(jnp.sum(centred * centred, axis=(0, 2)), "space") / cell_count
    inverse = lax.rsqrt(variance + norm_epsilon)
    whitened = centred * inverse[None, :, None]
    normed = norm_gain[None, :, None] * whitened + norm_shift[None, :, None]
    pooled = pool_slab(leaky_relu(normed), planes, GRID).astype(jnp.bfloat16)
    samples_pooled = lax.all_to_all(pooled, "space", split_axis=0, concat_axis=2, tiled=True)

    def second_conv(volume):
        return jnp.dot(
            conv_out,
            columns(pad_planes(volume, half_grid), half_grid, half_grid),
            preferred_element_type=jnp.float32,
        )

    second_out = lax.map(second_conv, samples_pooled)
    local_samples = second_out.shape[0]
    features = (
        pool_slab(leaky_relu(second_out), half_grid, half_grid)
        .reshape(local_samples, -1)
        .astype(jnp.bfloat16)
    )
    hidden_pre = jnp.dot(features, dense_in, preferred_element_type=jnp.float32)
    hidden = leaky_relu(hidden_pre).astype(jnp.bfloat16)
    predictions = jnp.dot(hidden, dense_out, preferred_element_type=jnp.float32)
    misfit = predictions - targets
    grad_out_local = jnp.dot(hidden.astype(jnp.float32).T, misfit, precision=lax.Precision.HIGHEST)
    back_hidden = (
        jnp.dot(misfit, dense_out.astype(jnp.float32).T, precision=lax.Precision.HIGHEST)
        * slope_of(hidden_pre)
    ).astype(jnp.bfloat16)
    partial_rows = lax.psum_scatter(
        lax.dot_general(
            features, back_hidden, (((0,), (0,)), ((), ())), preferred_element_type=jnp.float32
        ).astype(jnp.bfloat16),
        "dp",
        scatter_dimension=0,
        tiled=True,
    )
    grad_dense_in = lax.psum_scatter(partial_rows, "space", scatter_dimension=0, tiled=True).astype(
        jnp.float32
    )
    back_features = lax.dot_general(
        back_hidden, dense_in, (((1,), (1,)), ((), ())), preferred_element_type=jnp.float32
    )
    back_features = back_features.reshape(local_samples, C_OUT, quarter**3)
    back_second = (unpool_slab(back_features, half_grid, half_grid) * slope_of(second_out)).astype(
        jnp.bfloat16
    )

    def second_back(running, couple):
        volume, gradient = couple
        padded = pad_planes(volume, half_grid)
        patches = columns(padded, half_grid, half_grid)
        running = running + lax.dot_general(
            gradient, patches, (((1,), (1,)), ((), ())), preferred_element_type=jnp.float32
        )
        patch_grad = lax.dot_general(
            conv_out, gradient, (((0,), (0,)), ((), ())), preferred_element_type=jnp.float32
        )
        _, unfold = jax.vjp(
            lambda whole_pad: columns(whole_pad, half_grid, half_grid), padded.astype(jnp.float32)
        )
        volume_grad = unfold(patch_grad)[0][:, 1:-1, :]
        return (running, volume_grad.reshape(volume.shape).astype(jnp.bfloat16))

    grad_conv_out, back_pooled = lax.scan(
        second_back, jnp.zeros(conv_out.shape, jnp.float32), (samples_pooled, back_second)
    )
    back_slab = lax.all_to_all(back_pooled, "space", split_axis=2, concat_axis=0, tiled=True)
    back_active = unpool_slab(back_slab.astype(jnp.float32), planes, GRID) * slope_of(normed)
    sum_grad = jnp.sum(back_active, axis=(0, 2))
    sum_xgrad = jnp.sum(back_active * whitened, axis=(0, 2))
    group_grad, group_xgrad = lax.psum((sum_grad, sum_xgrad), "space")
    back_first = (norm_gain * inverse)[None, :, None] * (
        back_active
        - group_grad[None, :, None] / cell_count
        - whitened * group_xgrad[None, :, None] / cell_count
    )
    back_first = back_first.astype(jnp.bfloat16)

    def first_back(running, couple):
        slab_ext, gradient = couple
        patches = columns(slab_ext, planes, GRID)
        return (
            running
            + lax.dot_general(
                gradient, patches, (((1,), (1,)), ((), ())), preferred_element_type=jnp.float32
            ),
            None,
        )

    grad_conv_in, _ = lax.scan(
        first_back, jnp.zeros(conv_in.shape, jnp.float32), (extended, back_first)
    )
    grad_norm_local = jnp.stack([sum_xgrad, sum_grad])
    summed = lax.psum(
        (grad_conv_in, grad_norm_local, grad_conv_out, grad_out_local), ("dp", "space")
    )
    return (summed[0], summed[1], summed[2], grad_dense_in, summed[3], predictions)


def solution(mesh):
    placed = (P("dp", None, "space", None), P(), P(), P(), P(), P(), P(), P(("dp", "space"), None))
    return jax.shard_map(
        shards,
        mesh=mesh,
        in_specs=placed,
        out_specs=(P(), P(), P(), P(("dp", "space"), None), P(), P(("dp", "space"), None)),
        check_vma=False,
    )
```

profile of v0, /device:TPU:0, one launch (start us, length us, event | category | flops | bytes accessed | tf_op | source)
XLA Modules:
  0.0 1239.6 jit_solution(6425463289631794915)
XLA Ops:
  20.0 9.6 collective-permute-done
  34.9 9.2 pad_maximum_fusion
  44.1 170.7 %while.52 = (s32[]{:T(128)}, f32[8,64,8192]{2,1,0:T(8,128)}, bf16[8,32,10,1024]{3,2,1,0:T(8,128)(2,1)}, bf16[64,864]{1,0:T(8,128)(2,1)S(1)}, s32[]{:T(128)}) while((s32[]{:T(128)}, f32[8,64,8192]{2,1,0:T(8,128)}, bf16[8,32,10,1024]{3,2,1,0:T(8,128)(2,1)}, bf16[64,864]{1,0:T(8,128)(2,1)S(1)}, s32[]{:T(128)}) %tuple.218), condition=%wide.region_1.2_spmd, body=%wide.region_0.1_spmd.sunk | while | flops 934313984 | bytes 77505088 | solution.py:92
  52.5 8.8 copy.138
  116.5 8.8 copy.138
  137.8 8.8 copy.138
  159.2 8.8 copy.138
  214.8 23.5 %copy.52 = f32[8,64,8192]{1,0,2:T(8,128)} copy(f32[8,64,8192]{2,1,0:T(8,128)} %get-tuple-element.251) | data formatting | bytes 33554432 | tf_op jit(solution)/shard_map/while | solution.py:92
  245.2 9.9 psum.56
  255.2 15.0 %multiply_reduce_fusion.1 = f32[64]{0:T(128)S(1)} fusion(f32[8,64,8192]{1,0,2:T(8,128)} %copy.52, f32[64]{0:T(128)S(1)} %broadcast_multiply_fusion.1), kind=kLoop, calls=%fused_computation.417 | loop fusion | flops 12582848 | bytes 16777728 | tf_op jit(solution)/shard_map/reduce_sum | solution.py:96
  270.2 9.0 psum.57
  279.8 25.5 %fusion.222 = f32[8,64,8192]{1,0,2:T(8,128)} fusion(f32[8,64,8192]{1,0,2:T(8,128)} %copy.52, f32[64]{0:T(128)S(1)} %copy-done.23, f32[64]{0:T(128)S(1)} %get-tuple-element.447, f32[64]{0:T(128)S(1)} %copy-done.19, f32[64]{0:T(128)S(1)} %broadcast_multiply_fusion.1), kind=kLoop, calls=%fused_computation.415 | loop fusion | flops 33554432 | bytes 33555456 | tf_op jit(solution)/shard_map/add | solution.py:29
  305.3 14.9 %reduce_sum.56 = f32[8,64,4,16,16]{1,0,4,3,2:T(8,128)} reduce(f32[8,64,4,2,16,2,16,2]{1,0,7,6,5,4,3,2:T(8,128)} %bitcast.865, f32[]{:T(128)} %constant.649.clone.1), dimensions={3,5,7}, to_apply=%region_6.7 | reduce | flops 3670016 | bytes 18874372 | tf_op jit(solution)/shard_map/reduce_sum | solution.py:70
  331.2 21.0 %all-to-all-done = bf16[8,64,1024]{2,1,0:T(8,128)(2,1)S(1)} async-done(((bf16[8,64,1024]{2,1,0:T(8,128)(2,1)}), bf16[8,64,1024]{2,1,0:T(8,128)(2,1)S(1)}, u32[]{:S(2)}, u32[]{:S(2)}) %all-to-all-start) | async-done | bytes 1048608 | tf_op jit(solution)/shard_map/all_to_all | solution.py:101
  352.4 35.7 %while.53 = (s32[]{:T(128)}, f32[2,128,4096]{1,2,0:T(8,128)}, bf16[2,64,4096]{2,1,0:T(8,128)(2,1)S(1)}, bf16[128,1728]{0,1:T(8,128)(2,1)S(1)}, s32[]{:T(128)}) while((s32[]{:T(128)}, f32[2,128,4096]{1,2,0:T(8,128)}, bf16[2,64,4096]{2,1,0:T(8,128)(2,1)S(1)}, bf16[128,1728]{0,1:T(8,128)(2,1)S(1)}, s32[]{:T(128)}) %tuple.217), condition=%wide.region_8.9_spmd, body=%wide.region_7.8_spmd.sunk | while | flops 1840259072 | bytes 77004352 | solution.py:110
  419.6 10.2 convolution_multiply_fusion
  429.8 9.3 convolution_convert_fusion
  458.9 268.3 %while.54 = (s32[]{:T(128)}, f32[128,1728]{0,1:T(8,128)}, bf16[2,64,4096]{2,1,0:T(8,128)(2,1)}, bf16[2,128,4096]{1,2,0:T(8,128)(2,1)S(1)}, bf16[2,64,4096]{2,1,0...) while((s32[]{:T(128)}, f32[128,1728]{0,1:T(8,128)}, ...), condition=%wide.region_11.12_spmd.clone, body=%wide.region_10.11_spmd.clone.sunk | while | flops 3666803200 | bytes 362422176 | solution.py:161
  481.5 12.6 %convolution_bitcast_fusion.4 = f32[1728,4096]{1,0:T(8,128)} fusion(bf16[128,1728]{0,1:T(8,128)(2,1)} %get-tuple-element.749, bf16[2,128,4096]{1,2,0:T(8,128)(2,1)S(1)} %get-tuple-element.747, s32[]{:T(128)} %get-tuple-element.736), kind=kOutput, calls=%fused_computation.158.clone.1 | convolution fusion | flops 1811939328 | bytes 29802500 | tf_op jit(solution)/shard_map/while/body/eval_jaxpr/dot_general | solution.py:152
  494.1 10.4 fusion.376
  582.9 9.4 copy.169
  602.1 12.2 convolution_bitcast_fusion.4
  614.3 9.8 fusion.376
  701.2 9.4 copy.169
  738.6 23.6 %all-to-all-done.1 = bf16[4,2,65536]{2,1,0:T(2,128)(2,1)S(1)} async-done(((bf16[4,2,65536]{2,1,0:T(2,128)(2,1)}), bf16[4,2,65536]{2,1,0:T(2,128)(2,1)S(1)}, u32[]{:S(2)}, u32[]{:S(2)}) %all-to-all-start.1) | async-done | bytes 1048608 | tf_op jit(solution)/shard_map/all_to_all | solution.py:164
  778.5 22.3 %fusion.223 = (f32[64]{0:T(128)S(1)}, f32[64]{0:T(128)S(1)}) fusion(f32[8,64,8192]{1,0,2:T(8,128)} %copy.52, f32[8,64,4,16,16]{1,0,4,3,2:T(8,128)S(1)} %copy.62, f32[64]{0:T(128)S(1)} %copy-done.24, f32[64]{0:T(128)S(1)} %copy-done.22, f32[64]{0:T(128)S(1)} %copy-done.20, f32[64]{0:T(128)S(1)} %copy-done.18), kind=kLoop, calls=%fused_computation.419 | loop fusion | flops 58720128 | bytes 18875904 | tf_op jit(solution)/shard_map/reduce_sum | solution.py:166
  800.8 9.8 all-reduce.43
  810.6 25.9 %multiply_convert_fusion = bf16[8,64,8192]{1,0,2:T(8,128)(2,1)} fusion(f32[8,64,8192]{1,0,2:T(8,128)} %copy.52, f32[64]{0:T(128)S(1)} %get-tuple-element.374, f32[64]{0:T(128)S(1)} %broadcast_multiply_fusion, f32[8,64,4,16,16]{1,0,4,3,2:T(8,128)} %copy-done.11, f32[64]{0:T(128)S(1)} %copy-done.24, f32[64]{0:T(128)S(1)} %copy-done.22, f32[64]{0:T(128)S(1)} %copy-done.20, ...), kind=kLoop, calls=%fused_computation.412 | loop fusion | flops 71303168 | bytes 27264768 | tf_op jit(solution)/shard_map/convert_element_type | solution.py:174
  836.5 18.4 %copy.63 = bf16[8,64,8192]{2,1,0:T(8,128)(2,1)} copy(bf16[8,64,8192]{1,0,2:T(8,128)(2,1)} %multiply_convert_fusion) | data formatting | bytes 16777216
  855.0 242.5 %while.55 = (s32[]{:T(128)}, f32[64,864]{1,0:T(8,128)S(1)}, bf16[8,64,8192]{2,1,0:T(8,128)(2,1)}, bf16[8,32,10,1024]{3,2,1,0:T(8,128)(2,1)}, s32[]{:T(128)}, /*index=5*/s32[]{:T(128)}) while((s32[]{:T(128)}, f32[64,864]{1,0:T(8,128)S(1)}, bf16[8,64,8192]{2,1,0:T(8,128)(2,1)}, bf16[8,32,10,1024]{3,2,1,0:T(8,128)(2,1)}, ...), condition=%wide.region_17.18_spmd.clone, body=%wide.region_16.17_spmd.clone.sunk | while | flops 934424576 | bytes 76788304 | solution.py:187
  863.6 12.1 copy.170
  875.8 9.8 convolution_add_fusion.5
  894.0 12.1 copy.170
  906.2 9.7 convolution_add_fusion.5
  924.3 12.1 copy.170
  936.4 9.7 convolution_add_fusion.5
  954.6 12.1 copy.170
  966.7 9.7 convolution_add_fusion.5
  984.9 12.1 copy.170
  997.0 9.7 convolution_add_fusion.5
  1015.1 12.1 copy.170
  1027.3 9.7 convolution_add_fusion.5
  1045.4 12.1 copy.170
  1057.6 9.7 convolution_add_fusion.5
  1075.7 12.1 copy.170
  1087.8 9.7 convolution_add_fusion.5
  1098.5 39.9 %all-reduce.41 = (f32[2,64]{1,0:T(2,128)}, f32[128,4]{0,1:T(4,128)}) all-reduce(f32[2,64]{1,0:T(2,128)S(1)} %pad_maximum_fusion.1, f32[128,4]{0,1:T(4,128)S(1)} %fusion.228), channel_id=1, replica_groups=mesh['dp'=8,'space'=4] {'dp','space'}, use_global_device_ids=true, to_apply=%region_19.20 | all-reduce | flops 640 | bytes 5120 | tf_op jit(solution)/shard_map/psum | solution.py:191
  1140.5 87.6 %all-reduce.46.cloned.1.call-done = (f32[64,864]{1,0:T(8,128)}, f32[128,1728]{0,1:T(8,128)}) async-done(((f32[64,864]{1,0:T(8,128)}, f32[128,1728]{0,1:T(8,128)}), (f32[64,864]{1,0:T(8,128)}, f32[128,1728]{0,1:T(8,128)})) %all-reduce.46.cloned.1.call-update) | async-done | bytes 1105936 | tf_op jit(solution)/shard_map/psum | solution.py:191
  (877 shorter events, 530.0 us)
Async XLA Ops:
  8.0 410.8 %copy-start = (bf16[128,4]{0,1:T(4,128)(2,1)S(1)}, bf16[128,4]{0,1:T(4,128)(2,1)}, u32[]{:S(2)}) copy-start(bf16[128,4]{0,1:T(4,128)(2,1)} %param.22) | copy-start | bytes 3076
  8.0 36.1 %copy-start.16 = (bf16[64,864]{1,0:T(8,128)(2,1)S(1)}, bf16[64,864]{1,0:T(8,128)(2,1)}, u32[]{:S(2)}) copy-start(bf16[64,864]{1,0:T(8,128)(2,1)} %param.17) | copy-start | bytes 331780
  13.6 16.1 %collective-permute-start = (bf16[8,32,1,1024]{3,1,2,0:T(8,128)(2,1)S(1)}, bf16[8,32,1,1024]{3,1,2,0:T(8,128)(2,1)S(1)}, u32[]{:S(2)}, u32[]{:S(2)}) collective-permute-start(bf16[8,32,1,1024]{3,1,2,0:T(8,128)(2,1)S(1)} %copy.67), channel_id=1, source_target_pairs={{0,1},{1,2},{2,3},{4,5},{5,6},{6,7},{8,9},{9,10},{10,11},{12,13},{... | collective-permute-start | bytes 1572872 | tf_op jit(solution)/shard_map/ppermute | solution.py:19
  18.7 15.3 %collective-permute-start.1 = (bf16[8,32,1,1024]{3,1,2,0:T(8,128)(2,1)S(1)}, bf16[8,32,1,1024]{3,1,2,0:T(8,128)(2,1)S(1)}, u32[]{:S(2)}, u32[]{:S(2)}) collective-permute-start(bf16[8,32,1,1024]{3,1,2,0:T(8,128)(2,1)S(1)} %copy.68), channel_id=1, source_target_pairs={{1,0},{2,1},{3,2},{5,4},{6,5},{7,6},{9,8},{10,9},{11,10},{13,12},{... | collective-permute-start | bytes 1572872 | tf_op jit(solution)/shard_map/ppermute | solution.py:21
  255.2 24.6 %copy-start.17 = (f32[64]{0:T(128)}, f32[64]{0:T(128)S(1)}, u32[]{:S(2)}) copy-start(f32[64]{0:T(128)S(1)} %broadcast_multiply_fusion.1) | copy-start | bytes 772
  255.2 24.1 %copy-start.19 = (f32[64]{0:T(128)S(1)}, f32[64]{0:T(128)}, u32[]{:S(2)}) copy-start(f32[64]{0:T(128)} %param.18) | copy-start | bytes 772
  255.2 24.6 %copy-start.23 = (f32[64]{0:T(128)S(1)}, f32[64]{0:T(128)}, u32[]{:S(2)}) copy-start(f32[64]{0:T(128)} %param.19) | copy-start | bytes 772
  279.8 25.5 %copy-start.21 = (f32[64]{0:T(128)}, f32[64]{0:T(128)S(1)}, u32[]{:S(2)}) copy-start(f32[64]{0:T(128)S(1)} %get-tuple-element.447) | copy-start | bytes 772
  305.3 47.0 %copy-start.14 = (bf16[128,1728]{0,1:T(8,128)(2,1)S(1)}, bf16[128,1728]{0,1:T(8,128)(2,1)}, u32[]{:S(2)}) copy-start(bf16[128,1728]{0,1:T(8,128)(2,1)} %param.20) | copy-start | bytes 1327108
  327.6 24.6 %all-to-all-start = ((bf16[8,64,1024]{2,1,0:T(8,128)(2,1)}), bf16[8,64,1024]{2,1,0:T(8,128)(2,1)S(1)}, u32[]{:S(2)}, u32[]{:S(2)}) async-start(bf16[8,64,1024]{2,1,0:T(8,128)(2,1)} %copy.54), calls=%async_computation | async-start | bytes 2097152 | tf_op jit(solution)/shard_map/all_to_all | solution.py:101
  331.2 523.7 %reduce-scatter.3.cloned.1.call-start = ((), (), s32[]{:S(2)}) async-start(), calls=%async_computation.4 | async-start | bytes 18874368 | tf_op jit(solution)/shard_map/reduce_scatter | solution.py:126
  404.7 14.8 %copy-start.28 = (f32[2,4]{1,0:T(2,128)S(1)}, f32[2,4]{1,0:T(2,128)}, u32[]{:S(2)}) copy-start(f32[2,4]{1,0:T(2,128)} %param.23) | copy-start | bytes 100
  479.8 1.0 copy-start.9
  479.8 1.7 copy-start.12
  519.4 11.2 copy-start.4
  519.4 12.5 %copy-start.3 = (f32[64,4096]{1,0:T(8,128)S(1)}, f32[64,4096]{1,0:T(8,128)}, u32[]{:S(2)}) copy-start(f32[64,4096]{1,0:T(8,128)} %get-tuple-element.634) | copy-start | bytes 3145732 | tf_op jit(solution)/shard_map/while
  520.7 12.6 %copy-start.2 = (f32[64,4096]{1,0:T(8,128)S(1)}, f32[64,4096]{1,0:T(8,128)}, u32[]{:S(2)}) copy-start(f32[64,4096]{1,0:T(8,128)} %get-tuple-element.635) | copy-start | bytes 3145732 | tf_op jit(solution)/shard_map/while
  530.6 9.5 copy-start.6
  530.6 10.8 copy-start.5
  531.9 10.8 copy-start.7
  533.2 9.4 copy-start.8
  582.8 9.4 copy-start.13
  592.3 8.2 copy-start.10
  600.4 1.0 copy-start.9
  600.4 1.6 copy-start.12
  638.6 10.8 copy-start.4
  638.6 12.1 copy-start.3
  639.9 12.2 copy-start.2
  649.4 9.5 copy-start.6
  649.4 10.8 copy-start.5
  650.7 10.7 copy-start.7
  652.1 9.4 copy-start.8
  701.2 9.4 copy-start.13
  710.6 8.4 copy-start.10
  734.9 27.2 %all-to-all-start.1 = ((bf16[4,2,65536]{2,1,0:T(2,128)(2,1)}), bf16[4,2,65536]{2,1,0:T(2,128)(2,1)S(1)}, u32[]{:S(2)}, u32[]{:S(2)}) async-start(bf16[4,2,65536]{2,1,0:T(2,128)(2,1)} %reshape.317), calls=%async_computation.1 | async-start | bytes 2097152 | tf_op jit(solution)/shard_map/all_to_all | solution.py:164
  738.5 400.0 %reduce-scatter.5.cloned.1.call-start = ((), (), s32[]{:S(2)}) async-start(), calls=%async_computation.5 | async-start | bytes 2621440 | tf_op jit(solution)/shard_map/reduce_scatter | solution.py:134
  738.5 39.9 %copy-start.18 = (f32[64]{0:T(128)S(1)}, f32[64]{0:T(128)}, u32[]{:S(2)}) copy-start(f32[64]{0:T(128)} %copy-done.17) | copy-start | bytes 772
  738.5 39.9 %copy-start.20 = (f32[64]{0:T(128)S(1)}, f32[64]{0:T(128)}, u32[]{:S(2)}) copy-start(f32[64]{0:T(128)} %param.18) | copy-start | bytes 772
  738.5 39.9 %copy-start.22 = (f32[64]{0:T(128)S(1)}, f32[64]{0:T(128)}, u32[]{:S(2)}) copy-start(f32[64]{0:T(128)} %copy-done.21) | copy-start | bytes 772
  738.6 39.9 %copy-start.24 = (f32[64]{0:T(128)S(1)}, f32[64]{0:T(128)}, u32[]{:S(2)}) copy-start(f32[64]{0:T(128)} %param.19) | copy-start | bytes 772
  778.5 22.3 %copy-start.11 = (f32[8,64,4,16,16]{1,0,4,3,2:T(8,128)}, f32[8,64,4,16,16]{1,0,4,3,2:T(8,128)S(1)}, u32[]{:S(2)}) copy-start(f32[8,64,4,16,16]{1,0,4,3,2:T(8,128)S(1)} %copy.62) | copy-start | bytes 6291460
  778.5 32.2 %copy-start.25 = (f32[64]{0:T(128)S(1)}, f32[64]{0:T(128)}, u32[]{:S(2)}) copy-start(f32[64]{0:T(128)} %get-tuple-element.446) | copy-start | bytes 772
  854.9 373.2 %all-reduce.46.cloned.1.call-start = ((), (), s32[]{:S(2)}) async-start(), calls=%async_computation.6 | async-start | bytes 2228224 | tf_op jit(solution)/shard_map/psum | solution.py:191
  855.0 243.3 %copy-start.27 = (bf16[2,128]{1,0:T(2,128)(2,1)S(1)}, bf16[2,128]{1,0:T(2,128)(2,1)}, u32[]{:S(2)}) copy-start(bf16[2,128]{1,0:T(2,128)(2,1)} %copy-done.26) | copy-start | bytes 1540
  855.0 243.3 %copy-start.29 = (f32[2,4]{1,0:T(2,128)S(1)}, f32[2,4]{1,0:T(2,128)}, u32[]{:S(2)}) copy-start(f32[2,4]{1,0:T(2,128)} %param.23) | copy-start | bytes 100
  855.0 243.3 %copy-start.31 = (f32[2,4]{1,0:T(2,128)S(1)}, f32[2,4]{1,0:T(2,128)}, u32[]{:S(2)}) copy-start(f32[2,4]{1,0:T(2,128)} %copy-done.30) | copy-start | bytes 100
  1097.6 0.7 copy-start.15
  1097.6 134.3 %copy-start.1 = (bf16[128,4]{0,1:T(4,128)(2,1)S(1)}, bf16[128,4]{0,1:T(4,128)(2,1)}, u32[]{:S(2)}) copy-start(bf16[128,4]{0,1:T(4,128)(2,1)} %param.22) | copy-start | bytes 3076
  (2 other events, 1.2 us)
Sparse Core Ops, SparseCore 0:
  459.0 115.2 reduce-scatter.2
  855.0 42.4 reduce-scatter.4
Sparse Core Ops, SparseCore 1:
  1098.4 129.7 all-reduce.45
where the time goes:
time: 1250 us; the launch traced here: 1240 us
  local copies, waits for them, and re-layouts  443 us (35%)
  other arithmetic  328 us (26%)
  matrix products  190 us (15%)
  waiting for transfers between devices  145 us (12%)
  blocking collectives  68.7 us (5%)
  loops' own time  34.6 us (3%)
  between operations  16.2 us (1%)
  starting transfers between devices  13.4 us (1%)
    while x122, local copies, waits for them, and re-layouts  269 us
    while x520, other arithmetic  123 us
    psum x1, waiting for transfers between devices, shards(): lax.psum((grad_conv_in, grad_norm_local, grad_conv_out, grad_out_local),...  87.6 us
    dot_general x8, matrix products, first_back(): lax.dot_general(gradient, patches, (((1,), (1,)), ((), ())), preferred_el...  77.7 us
    psum x1, blocking collectives, shards(): lax.psum((grad_conv_in, grad_norm_local, grad_conv_out, grad_out_local),...  39.9 us
    dot_general x8, matrix products, first_conv(): jnp.dot(conv_in, columns(slab_ext, planes, GRID), preferred_element_type=...  32.8 us
    another operation x4, local copies, waits for them, and re-layouts, columns(): stacked = jnp.stack(pieces, 0)  31.5 us
    add x2, other arithmetic, leaky_relu(): return 0.65 * values + 0.35 * values * jnp.tanh(values)  30.5 us
  transfers between devices with their start and end apart: 7, of which 5 were waited for; matrix products, arithmetic and copies ran while one was open for 46% of the time, Pallas kernels for 0%

commit v1 on v0

--- a/solution.py
+++ b/solution.py
@@ -188,9 +188,9 @@
         first_back, jnp.zeros(conv_in.shape, jnp.float32), (extended, back_first)
     )
     grad_norm_local = jnp.stack([sum_xgrad, sum_grad])
-    summed = lax.psum(
-        (grad_conv_in, grad_norm_local, grad_conv_out, grad_out_local), ("dp", "space")
-    )
+    summed = (grad_conv_in, grad_norm_local, grad_conv_out, grad_out_local)
+    for mesh_axis in ("space", "dp"):
+        summed = lax.psum(summed, mesh_axis)
     return (summed[0], summed[1], summed[2], grad_dense_in, summed[3], predictions)
 
 

time: 1250 us -> 1220 us (0.976)
  blocking collectives: 68.7 us -> 43.4 us
    reduce_scatter x1, waiting for transfers between devices: 0.01 us -> 30.7 us  [shards(): lax.psum_scatter(partial_rows, 'space', scatter_dimension=0, tiled=True)]
    psum x1 -> x2, waiting for transfers between devices: 87.6 us -> 62.1 us  [shards(): summed = lax.psum(summed, mesh_axis)]
    psum x1, blocking collectives: 39.9 us -> 14.4 us  [shards(): summed = lax.psum(summed, mesh_axis)]
    all_to_all x1, waiting for transfers between devices: 23.6 us -> 10.9 us  [shards(): lax.all_to_all(back_pooled, 'space', split_axis=2, concat_axis=0, tiled=T...]
    unnamed x49 -> x55, local copies, waits for them, and re-layouts: 28 us -> 28.8 us
  transfers between devices with their start and end apart: 7 -> 8, of which waited for: 5 -> 7; matrix products, arithmetic and copies ran while one was open for 46% -> 28% of each run, Pallas kernels for 0% -> 0%
where the time goes in v1:
time: 1220 us; the launch traced here: 1210 us
  local copies, waits for them, and re-layouts  444 us (36%)
  other arithmetic  328 us (27%)
  matrix products  192 us (16%)
  waiting for transfers between devices  138 us (11%)
  blocking collectives  43.4 us (4%)
  loops' own time  34.4 us (3%)
  between operations  16.1 us (1%)
  starting transfers between devices  13.5 us (1%)
    while x122, local copies, waits for them, and re-layouts  269 us
    while x520, other arithmetic  123 us
    dot_general x8, matrix products, first_back(): lax.dot_general(gradient, patches, (((1,), (1,)), ((), ())), preferred_el...  77.6 us
    psum x2, waiting for transfers between devices, shards(): summed = lax.psum(summed, mesh_axis)  62.1 us
    dot_general x8, matrix products, first_conv(): jnp.dot(conv_in, columns(slab_ext, planes, GRID), preferred_element_type=...  32.8 us
    reduce_scatter x1, waiting for transfers between devices, shards(): lax.psum_scatter(partial_rows, 'space', scatter_dimension=0, tiled=True)  30.7 us
    another operation x4, local copies, waits for them, and re-layouts, columns(): stacked = jnp.stack(pieces, 0)  30.5 us
    add x2, other arithmetic, leaky_relu(): return 0.65 * values + 0.35 * values * jnp.tanh(values)  30.5 us
  transfers between devices with their start and end apart: 8, of which 7 were waited for; matrix products, arithmetic and copies ran while one was open for 28% of the time, Pallas kernels for 0%

profile of v1, /device:TPU:0, one launch (start us, length us, event | category | flops | bytes accessed | tf_op | source)
XLA Modules:
  0.0 1208.9 jit_solution(4057913297306282948)
XLA Ops:
  20.0 9.6 collective-permute-done
  34.8 9.2 pad_maximum_fusion
  44.0 170.8 %while.52 = (s32[]{:T(128)}, f32[8,64,8192]{2,1,0:T(8,128)}, bf16[8,32,10,1024]{3,2,1,0:T(8,128)(2,1)}, bf16[64,864]{1,0:T(8,128)(2,1)S(1)}, s32[]{:T(128)}) while((s32[]{:T(128)}, f32[8,64,8192]{2,1,0:T(8,128)}, bf16[8,32,10,1024]{3,2,1,0:T(8,128)(2,1)}, bf16[64,864]{1,0:T(8,128)(2,1)S(1)}, s32[]{:T(128)}) %tuple.221), condition=%wide.region_1.2_spmd, body=%wide.region_0.1_spmd.sunk | while | flops 934313984 | bytes 77505088 | solution.py:92
  52.5 8.8 copy.138
  116.4 8.8 copy.138
  214.8 23.5 %copy.52 = f32[8,64,8192]{1,0,2:T(8,128)} copy(f32[8,64,8192]{2,1,0:T(8,128)} %get-tuple-element.251) | data formatting | bytes 33554432 | tf_op jit(solution)/shard_map/while | solution.py:92
  245.2 9.9 psum.84
  255.1 15.0 %multiply_reduce_fusion.1 = f32[64]{0:T(128)S(1)} fusion(f32[8,64,8192]{1,0,2:T(8,128)} %copy.52, f32[64]{0:T(128)S(1)} %broadcast_multiply_fusion.1), kind=kLoop, calls=%fused_computation.417 | loop fusion | flops 12582848 | bytes 16777728 | tf_op jit(solution)/shard_map/reduce_sum | solution.py:96
  270.2 9.0 psum.85
  279.7 25.6 %fusion.222 = f32[8,64,8192]{1,0,2:T(8,128)} fusion(f32[8,64,8192]{1,0,2:T(8,128)} %copy.52, f32[64]{0:T(128)S(1)} %copy-done.24, f32[64]{0:T(128)S(1)} %get-tuple-element.451, f32[64]{0:T(128)S(1)} %copy-done.20, f32[64]{0:T(128)S(1)} %broadcast_multiply_fusion.1), kind=kLoop, calls=%fused_computation.415 | loop fusion | flops 33554432 | bytes 33555456 | tf_op jit(solution)/shard_map/add | solution.py:29
  305.3 15.0 %reduce_sum.56 = f32[8,64,4,16,16]{1,0,4,3,2:T(8,128)} reduce(f32[8,64,4,2,16,2,16,2]{1,0,7,6,5,4,3,2:T(8,128)} %bitcast.865, f32[]{:T(128)} %constant.649.clone.1), dimensions={3,5,7}, to_apply=%region_6.7 | reduce | flops 3670016 | bytes 18874372 | tf_op jit(solution)/shard_map/reduce_sum | solution.py:70
  331.2 21.1 %all-to-all-done = bf16[8,64,1024]{2,1,0:T(8,128)(2,1)S(1)} async-done(((bf16[8,64,1024]{2,1,0:T(8,128)(2,1)}), bf16[8,64,1024]{2,1,0:T(8,128)(2,1)S(1)}, u32[]{:S(2)}, u32[]{:S(2)}) %all-to-all-start) | async-done | bytes 1048608 | tf_op jit(solution)/shard_map/all_to_all | solution.py:101
  352.4 35.7 %while.53 = (s32[]{:T(128)}, f32[2,128,4096]{1,2,0:T(8,128)}, bf16[2,64,4096]{2,1,0:T(8,128)(2,1)S(1)}, bf16[128,1728]{0,1:T(8,128)(2,1)S(1)}, s32[]{:T(128)}) while((s32[]{:T(128)}, f32[2,128,4096]{1,2,0:T(8,128)}, bf16[2,64,4096]{2,1,0:T(8,128)(2,1)S(1)}, bf16[128,1728]{0,1:T(8,128)(2,1)S(1)}, s32[]{:T(128)}) %tuple.220), condition=%wide.region_8.9_spmd, body=%wide.region_7.8_spmd.sunk | while | flops 1840259072 | bytes 77004352 | solution.py:110
  419.8 10.2 convolution_multiply_fusion
  449.7 266.0 %while.54 = (s32[]{:T(128)}, f32[128,1728]{0,1:T(8,128)}, bf16[2,64,4096]{2,1,0:T(8,128)(2,1)}, bf16[2,128,4096]{1,2,0:T(8,128)(2,1)S(1)}, bf16[2,64,4096]{2,1,0...) while((s32[]{:T(128)}, f32[128,1728]{0,1:T(8,128)}, ...), condition=%wide.region_11.12_spmd.clone, body=%wide.region_10.11_spmd.clone.sunk | while | flops 3666803200 | bytes 362422176 | solution.py:161
  472.3 12.2 %convolution_bitcast_fusion.4 = f32[1728,4096]{1,0:T(8,128)} fusion(bf16[128,1728]{0,1:T(8,128)(2,1)} %get-tuple-element.753, bf16[2,128,4096]{1,2,0:T(8,128)(2,1)S(1)} %get-tuple-element.751, s32[]{:T(128)} %get-tuple-element.740), kind=kOutput, calls=%fused_computation.158.clone.1 | convolution fusion | flops 1811939328 | bytes 29802500 | tf_op jit(solution)/shard_map/while/body/eval_jaxpr/dot_general | solution.py:152
  484.6 9.7 fusion.376
  571.3 9.4 copy.169
  590.6 12.2 %convolution_bitcast_fusion.4 = f32[1728,4096]{1,0:T(8,128)} fusion(bf16[128,1728]{0,1:T(8,128)(2,1)} %get-tuple-element.753, bf16[2,128,4096]{1,2,0:T(8,128)(2,1)S(1)} %get-tuple-element.751, s32[]{:T(128)} %get-tuple-element.740), kind=kOutput, calls=%fused_computation.158.clone.1 | convolution fusion | flops 1811939328 | bytes 29802500 | tf_op jit(solution)/shard_map/while/body/eval_jaxpr/dot_general | solution.py:152
  602.9 9.7 fusion.376
  689.6 9.4 copy.169
  727.0 10.8 convolution_convert_fusion
  738.7 10.9 all-to-all-done.1
  767.0 22.5 %fusion.223 = (f32[64]{0:T(128)S(1)}, f32[64]{0:T(128)S(1)}) fusion(f32[8,64,8192]{1,0,2:T(8,128)} %copy.52, f32[8,64,4,16,16]{1,0,4,3,2:T(8,128)S(1)} %copy.62, f32[64]{0:T(128)S(1)} %copy-done.25, f32[64]{0:T(128)S(1)} %copy-done.23, f32[64]{0:T(128)S(1)} %copy-done.21, f32[64]{0:T(128)S(1)} %copy-done.19), kind=kLoop, calls=%fused_computation.419 | loop fusion | flops 58720128 | bytes 18875904 | tf_op jit(solution)/shard_map/reduce_sum | solution.py:166
  789.6 10.1 all-reduce.43
  799.6 26.1 %multiply_convert_fusion = bf16[8,64,8192]{1,0,2:T(8,128)(2,1)} fusion(f32[8,64,8192]{1,0,2:T(8,128)} %copy.52, f32[64]{0:T(128)S(1)} %get-tuple-element.374, f32[64]{0:T(128)S(1)} %broadcast_multiply_fusion, f32[8,64,4,16,16]{1,0,4,3,2:T(8,128)} %copy-done.11, f32[64]{0:T(128)S(1)} %copy-done.25, f32[64]{0:T(128)S(1)} %copy-done.23, f32[64]{0:T(128)S(1)} %copy-done.21, ...), kind=kLoop, calls=%fused_computation.412 | loop fusion | flops 71303168 | bytes 27264768 | tf_op jit(solution)/shard_map/convert_element_type | solution.py:174
  825.7 18.6 %copy.63 = bf16[8,64,8192]{2,1,0:T(8,128)(2,1)} copy(bf16[8,64,8192]{1,0,2:T(8,128)(2,1)} %multiply_convert_fusion) | data formatting | bytes 16777216
  844.3 242.4 %while.55 = (s32[]{:T(128)}, f32[64,864]{1,0:T(8,128)S(1)}, bf16[8,64,8192]{2,1,0:T(8,128)(2,1)}, bf16[8,32,10,1024]{3,2,1,0:T(8,128)(2,1)}, s32[]{:T(128)}, /*index=5*/s32[]{:T(128)}) while((s32[]{:T(128)}, f32[64,864]{1,0:T(8,128)S(1)}, bf16[8,64,8192]{2,1,0:T(8,128)(2,1)}, bf16[8,32,10,1024]{3,2,1,0:T(8,128)(2,1)}, ...), condition=%wide.region_17.18_spmd.clone, body=%wide.region_16.17_spmd.clone.sunk | while | flops 934424576 | bytes 76788304 | solution.py:187
  852.8 12.2 %copy.170 = bf16[108,8,8,1024]{3,1,2,0:T(8,128)(2,1)} copy(bf16[108,8,8,1024]{3,2,1,0:T(8,128)(2,1)S(1)} %bitcast.862) | data formatting | bytes 28311552 | tf_op jit(solution)/shard_map/while
  865.0 9.7 convolution_add_fusion.5
  883.1 12.2 %copy.170 = bf16[108,8,8,1024]{3,1,2,0:T(8,128)(2,1)} copy(bf16[108,8,8,1024]{3,2,1,0:T(8,128)(2,1)S(1)} %bitcast.862) | data formatting | bytes 28311552 | tf_op jit(solution)/shard_map/while
  895.3 9.7 convolution_add_fusion.5
  913.4 12.2 %copy.170 = bf16[108,8,8,1024]{3,1,2,0:T(8,128)(2,1)} copy(bf16[108,8,8,1024]{3,2,1,0:T(8,128)(2,1)S(1)} %bitcast.862) | data formatting | bytes 28311552 | tf_op jit(solution)/shard_map/while
  925.6 9.7 convolution_add_fusion.5
  943.7 12.2 %copy.170 = bf16[108,8,8,1024]{3,1,2,0:T(8,128)(2,1)} copy(bf16[108,8,8,1024]{3,2,1,0:T(8,128)(2,1)S(1)} %bitcast.862) | data formatting | bytes 28311552 | tf_op jit(solution)/shard_map/while
  955.9 9.7 convolution_add_fusion.5
  974.0 12.2 %copy.170 = bf16[108,8,8,1024]{3,1,2,0:T(8,128)(2,1)} copy(bf16[108,8,8,1024]{3,2,1,0:T(8,128)(2,1)S(1)} %bitcast.862) | data formatting | bytes 28311552 | tf_op jit(solution)/shard_map/while
  986.2 9.7 convolution_add_fusion.5
  1004.3 12.2 %copy.170 = bf16[108,8,8,1024]{3,1,2,0:T(8,128)(2,1)} copy(bf16[108,8,8,1024]{3,2,1,0:T(8,128)(2,1)S(1)} %bitcast.862) | data formatting | bytes 28311552 | tf_op jit(solution)/shard_map/while
  1016.4 9.7 convolution_add_fusion.5
  1034.6 12.2 %copy.170 = bf16[108,8,8,1024]{3,1,2,0:T(8,128)(2,1)} copy(bf16[108,8,8,1024]{3,2,1,0:T(8,128)(2,1)S(1)} %bitcast.862) | data formatting | bytes 28311552 | tf_op jit(solution)/shard_map/while
  1046.7 9.7 convolution_add_fusion.5
  1064.9 12.2 %copy.170 = bf16[108,8,8,1024]{3,1,2,0:T(8,128)(2,1)} copy(bf16[108,8,8,1024]{3,2,1,0:T(8,128)(2,1)S(1)} %bitcast.862) | data formatting | bytes 28311552 | tf_op jit(solution)/shard_map/while
  1077.0 9.7 convolution_add_fusion.5
  1088.1 52.7 %all-reduce.50.cloned.1.call-done = (f32[64,864]{1,0:T(8,128)}, f32[128,1728]{0,1:T(8,128)}) async-done(((f32[64,864]{1,0:T(8,128)}, f32[128,1728]{0,1:T(8,128)}), (f32[64,864]{1,0:T(8,128)}, f32[128,1728]{0,1:T(8,128)})) %all-reduce.50.cloned.1.call-update) | async-done | bytes 1105936 | tf_op jit(solution)/shard_map/psum | solution.py:193
  1140.8 14.4 %all-reduce.41 = (f32[2,64]{1,0:T(2,128)}, f32[128,4]{0,1:T(4,128)}) all-reduce(f32[2,64]{1,0:T(2,128)S(1)} %get-tuple-element.376, f32[128,4]{0,1:T(4,128)S(1)} %get-tuple-element.377), channel_id=1, replica_groups=mesh['dp'=8,'space'=4] {'dp'}, use_global_device_ids=true, to_apply=%region_21.22 | all-reduce | flops 640 | bytes 5120 | tf_op jit(solution)/shard_map/psum | solution.py:193
  1155.2 30.7 %reduce-scatter.5.cloned.1.call-done = bf16[2048,128]{1,0:T(8,128)(2,1)} async-done(((bf16[8192,128]{1,0:T(8,128)(2,1)}), bf16[2048,128]{1,0:T(8,128)(2,1)}) %reduce-scatter.5.cloned.1.call-update) | async-done | bytes 524304 | tf_op jit(solution)/shard_map/reduce_scatter | solution.py:134
  1188.0 9.4 all-reduce.48.cloned.1.call-done
  (886 shorter events, 548.7 us)
Async XLA Ops:
  8.0 411.0 %copy-start = (bf16[128,4]{0,1:T(4,128)(2,1)S(1)}, bf16[128,4]{0,1:T(4,128)(2,1)}, u32[]{:S(2)}) copy-start(bf16[128,4]{0,1:T(4,128)(2,1)} %param.22) | copy-start | bytes 3076
  8.0 36.0 %copy-start.17 = (bf16[64,864]{1,0:T(8,128)(2,1)S(1)}, bf16[64,864]{1,0:T(8,128)(2,1)}, u32[]{:S(2)}) copy-start(bf16[64,864]{1,0:T(8,128)(2,1)} %param.17) | copy-start | bytes 331780
  13.5 16.1 %collective-permute-start = (bf16[8,32,1,1024]{3,1,2,0:T(8,128)(2,1)S(1)}, bf16[8,32,1,1024]{3,1,2,0:T(8,128)(2,1)S(1)}, u32[]{:S(2)}, u32[]{:S(2)}) collective-permute-start(bf16[8,32,1,1024]{3,1,2,0:T(8,128)(2,1)S(1)} %copy.67), channel_id=1, source_target_pairs={{0,1},{1,2},{2,3},{4,5},{5,6},{6,7},{8,9},{9,10},{10,11},{12,13},{... | collective-permute-start | bytes 1572872 | tf_op jit(solution)/shard_map/ppermute | solution.py:19
  18.7 15.3 %collective-permute-start.1 = (bf16[8,32,1,1024]{3,1,2,0:T(8,128)(2,1)S(1)}, bf16[8,32,1,1024]{3,1,2,0:T(8,128)(2,1)S(1)}, u32[]{:S(2)}, u32[]{:S(2)}) collective-permute-start(bf16[8,32,1,1024]{3,1,2,0:T(8,128)(2,1)S(1)} %copy.68), channel_id=1, source_target_pairs={{1,0},{2,1},{3,2},{5,4},{6,5},{7,6},{9,8},{10,9},{11,10},{13,12},{... | collective-permute-start | bytes 1572872 | tf_op jit(solution)/shard_map/ppermute | solution.py:21
  255.1 24.6 %copy-start.18 = (f32[64]{0:T(128)}, f32[64]{0:T(128)S(1)}, u32[]{:S(2)}) copy-start(f32[64]{0:T(128)S(1)} %broadcast_multiply_fusion.1) | copy-start | bytes 772
  255.1 24.1 %copy-start.20 = (f32[64]{0:T(128)S(1)}, f32[64]{0:T(128)}, u32[]{:S(2)}) copy-start(f32[64]{0:T(128)} %param.18) | copy-start | bytes 772
  255.1 24.6 %copy-start.24 = (f32[64]{0:T(128)S(1)}, f32[64]{0:T(128)}, u32[]{:S(2)}) copy-start(f32[64]{0:T(128)} %param.19) | copy-start | bytes 772
  279.7 25.6 %copy-start.22 = (f32[64]{0:T(128)}, f32[64]{0:T(128)S(1)}, u32[]{:S(2)}) copy-start(f32[64]{0:T(128)S(1)} %get-tuple-element.451) | copy-start | bytes 772
  305.3 47.1 %copy-start.14 = (bf16[128,1728]{0,1:T(8,128)(2,1)S(1)}, bf16[128,1728]{0,1:T(8,128)(2,1)}, u32[]{:S(2)}) copy-start(bf16[128,1728]{0,1:T(8,128)(2,1)} %param.20) | copy-start | bytes 1327108
  327.7 24.6 %all-to-all-start = ((bf16[8,64,1024]{2,1,0:T(8,128)(2,1)}), bf16[8,64,1024]{2,1,0:T(8,128)(2,1)S(1)}, u32[]{:S(2)}, u32[]{:S(2)}) async-start(bf16[8,64,1024]{2,1,0:T(8,128)(2,1)} %copy.54), calls=%async_computation | async-start | bytes 2097152 | tf_op jit(solution)/shard_map/all_to_all | solution.py:101
  404.8 14.9 %copy-start.31 = (f32[2,4]{1,0:T(2,128)S(1)}, f32[2,4]{1,0:T(2,128)}, u32[]{:S(2)}) copy-start(f32[2,4]{1,0:T(2,128)} %param.23) | copy-start | bytes 100
  411.5 18.5 %copy-start.16 = (bf16[2,65536]{1,0:T(2,128)(2,1)}, bf16[2,65536]{1,0:T(2,128)(2,1)S(1)}, u32[]{:S(2)}) copy-start(bf16[2,65536]{1,0:T(2,128)(2,1)S(1)} %convert_element_type.690) | copy-start | bytes 786436
  419.8 18.3 %copy-start.26 = (bf16[2,128]{1,0:T(2,128)(2,1)}, bf16[2,128]{1,0:T(2,128)(2,1)S(1)}, u32[]{:S(2)}) copy-start(bf16[2,128]{1,0:T(2,128)(2,1)S(1)} %fusion.225) | copy-start | bytes 1540
  449.7 277.3 %copy-start.27 = (bf16[2,128]{1,0:T(2,128)(2,1)S(1)}, bf16[2,128]{1,0:T(2,128)(2,1)}, u32[]{:S(2)}) copy-start(bf16[2,128]{1,0:T(2,128)(2,1)} %copy-done.26) | copy-start | bytes 1540
  470.6 1.0 copy-start.9
  470.6 1.7 copy-start.12
  508.9 10.8 copy-start.4
  508.9 12.1 %copy-start.3 = (f32[64,4096]{1,0:T(8,128)S(1)}, f32[64,4096]{1,0:T(8,128)}, u32[]{:S(2)}) copy-start(f32[64,4096]{1,0:T(8,128)} %get-tuple-element.638) | copy-start | bytes 3145732 | tf_op jit(solution)/shard_map/while
  510.2 12.1 copy-start.2
  519.7 9.4 copy-start.6
  519.7 10.7 copy-start.5
  521.0 10.7 copy-start.7
  522.3 9.4 copy-start.8
  571.3 9.5 copy-start.13
  580.8 8.2 copy-start.10
  588.9 1.0 copy-start.9
  588.9 1.7 copy-start.12
  627.2 10.8 copy-start.4
  627.2 12.1 %copy-start.3 = (f32[64,4096]{1,0:T(8,128)S(1)}, f32[64,4096]{1,0:T(8,128)}, u32[]{:S(2)}) copy-start(f32[64,4096]{1,0:T(8,128)} %get-tuple-element.638) | copy-start | bytes 3145732 | tf_op jit(solution)/shard_map/while
  628.5 12.1 copy-start.2
  638.0 9.4 copy-start.6
  638.0 10.7 copy-start.5
  639.3 10.7 copy-start.7
  640.6 9.4 copy-start.8
  689.6 9.5 copy-start.13
  699.1 8.4 copy-start.10
  723.4 26.3 %all-to-all-start.1 = ((bf16[4,2,65536]{2,1,0:T(2,128)(2,1)}), bf16[4,2,65536]{2,1,0:T(2,128)(2,1)S(1)}, u32[]{:S(2)}, u32[]{:S(2)}) async-start(bf16[4,2,65536]{2,1,0:T(2,128)(2,1)} %reshape.317), calls=%async_computation.1 | async-start | bytes 2097152 | tf_op jit(solution)/shard_map/all_to_all | solution.py:164
  726.9 360.6 %reduce-scatter.3.cloned.1.call-start = ((), (), s32[]{:S(2)}) async-start(), calls=%async_computation.4 | async-start | bytes 18874368 | tf_op jit(solution)/shard_map/reduce_scatter | solution.py:126
  737.9 402.9 %all-reduce.50.cloned.1.call-start = ((), (), s32[]{:S(2)}) async-start(), calls=%async_computation.7 | async-start | bytes 2228224 | tf_op jit(solution)/shard_map/psum | solution.py:193
  738.7 28.2 %copy-start.19 = (f32[64]{0:T(128)S(1)}, f32[64]{0:T(128)}, u32[]{:S(2)}) copy-start(f32[64]{0:T(128)} %copy-done.18) | copy-start | bytes 772
  738.7 28.2 %copy-start.21 = (f32[64]{0:T(128)S(1)}, f32[64]{0:T(128)}, u32[]{:S(2)}) copy-start(f32[64]{0:T(128)} %param.18) | copy-start | bytes 772
  738.7 28.2 %copy-start.23 = (f32[64]{0:T(128)S(1)}, f32[64]{0:T(128)}, u32[]{:S(2)}) copy-start(f32[64]{0:T(128)} %copy-done.22) | copy-start | bytes 772
  738.7 28.2 %copy-start.25 = (f32[64]{0:T(128)S(1)}, f32[64]{0:T(128)}, u32[]{:S(2)}) copy-start(f32[64]{0:T(128)} %param.19) | copy-start | bytes 772
  767.0 22.5 %copy-start.11 = (f32[8,64,4,16,16]{1,0,4,3,2:T(8,128)}, f32[8,64,4,16,16]{1,0,4,3,2:T(8,128)S(1)}, u32[]{:S(2)}) copy-start(f32[8,64,4,16,16]{1,0,4,3,2:T(8,128)S(1)} %copy.62) | copy-start | bytes 6291460
  767.0 32.6 %copy-start.28 = (f32[64]{0:T(128)S(1)}, f32[64]{0:T(128)}, u32[]{:S(2)}) copy-start(f32[64]{0:T(128)} %get-tuple-element.450) | copy-start | bytes 772
  1086.7 114.5 %copy-start.1 = (bf16[128,4]{0,1:T(4,128)(2,1)S(1)}, bf16[128,4]{0,1:T(4,128)(2,1)}, u32[]{:S(2)}) copy-start(bf16[128,4]{0,1:T(4,128)(2,1)} %param.22) | copy-start | bytes 3076
  1087.5 98.4 %reduce-scatter.5.cloned.1.call-start = ((), (), s32[]{:S(2)}) async-start(), calls=%async_computation.5 | async-start | bytes 2621440 | tf_op jit(solution)/shard_map/reduce_scatter | solution.py:134
  1088.0 109.4 %all-reduce.48.cloned.1.call-start = ((), (), s32[]{:S(2)}) async-start(), calls=%async_computation.6 | async-start | bytes 2228224 | tf_op jit(solution)/shard_map/psum | solution.py:193
  (6 other events, 3.8 us)
Sparse Core Ops, SparseCore 0:
  738.0 117.5 reduce-scatter.2
  1140.9 56.4 all-reduce.47
Sparse Core Ops, SparseCore 1:
  1087.5 53.2 all-reduce.49
  1142.9 42.9 reduce-scatter.4
